TPU v7x, 256 devices: a whole 4x4x8 slice. The times are simulated.
256 devices in a mesh: row: 16 (over z, y_hi), col: 16 (over y_lo, x, core).
Axes of the slice: x: 4, y: 4 (y_hi: 2, y_lo: 2; y = y_hi * 2 + y_lo), z: 8, core: 2. Of those that a mesh axis runs over, the one named last changes fastest.
Arguments:
- anc_inverse: float32 [20480, 20480], P('row', 'col'), may hold values from -6 to 6
- l_store: float32 [16, 20480, 256], P('col', 'row'), may hold values from -0.0546875 to 0.0546875
- diag_inv: float32 [16, 256, 256], P('col'), may hold values from -6 to 6
- block_lists: int32 [4, 96], replicated, may hold values from 0 to 159, as said below
- block_counts: int32 [4], replicated, may hold values from 48 to 96, as said below
- sibling_columns: int32 [4], replicated, may hold values from 0 to 15, as said below
Outputs:
- upper_out: float32 [4, 256, 20480], P(None, 'row', 'col')
- lower_out: float32 [16, 20480, 256], P('col', 'row')
- diag_out: float32 [16, 256, 256], P('col')
Inputs may be any that keep to these rules, and one draw needn't show every extreme that they name: `block_lists`: in each sibling's row the entries are distinct block indices; entries at positions from block_counts onward are ignored. `block_counts`: some sibling uses all 96 entries. `sibling_columns`: distinct columns for distinct siblings.
All inputs are finite; a program needn't handle non-finite values.
Results may differ from a plain program's by a relative error of at most 0.00011.
Values sent between devices are 32-bit elements; how exact they have to be, the bound alone decides.
No kernel may reach another device: no remote copies, remote signals or barrier semaphores. Data moves between devices by JAX's collectives and lax.ppermute only.
A program may use at most 64 MiB of HBM per device.

v0:
```python
import jax
import jax.numpy as jnp
from jax import lax
from jax.sharding import Mesh
from jax.sharding import PartitionSpec as P

BLK = 128
ROW = ("row_0", "row_1")


def padded_to(lines, length):
    spare = -len(lines) % length
    return jnp.pad(lines, [(0, spare)] + [(0, 0)] * (lines.ndim - 1))


def total_of(x, axis):
    lines = x.reshape(-1, *x.shape[1:][-1:])
    padded = padded_to(lines, lax.axis_size(axis))
    own = lax.psum_scatter(padded, axis, scatter_dimension=0, tiled=True)
    whole = lax.all_gather(own, axis, axis=0, tiled=True)
    return whole[: len(lines)].reshape(x.shape)


def summed_rows(x, axes, dim):
    if not axes:
        return x
    nearer = lax.psum_scatter(x, axes[0], scatter_dimension=dim, tiled=True)
    return summed_rows(nearer, axes[1:], dim)


def joined_along(parts, dim):
    shape = list(parts.shape[1:])
    shape[dim] *= parts.shape[0]
    return jnp.moveaxis(parts, 0, dim).reshape(shape)


def from_everyone(x, axis):
    length = lax.axis_size(axis)
    return lax.all_to_all(jnp.broadcast_to(x[None], (length, *x.shape)), axis, 0, 0, tiled=True)


def collect(x, axis, dim):
    return joined_along(from_everyone(x, axis), dim)


def cut_along(x, dim, length):
    shape = x.shape
    parts = x.reshape(*shape[:dim], length, shape[dim] // length, *shape[dim + 1 :])
    return jnp.moveaxis(parts, dim, 0)


def sum_at_owner(x, axis, dim):
    length = lax.axis_size(axis)
    parts = lax.all_to_all(cut_along(x, dim, length), axis, 0, 0, tiled=True)
    return jnp.sum(parts, axis=0)


def nested_sum(x, axes):
    lines = x.reshape(-1, x.shape[-1])
    padded = padded_to(lines, lax.axis_size(axes))
    whole = collect(sum_at_owner(padded, axes, 0), axes, 0)
    return lax.slice_in_dim(whole, 0, len(lines)).reshape(x.shape)


def listed_blocks(block_lists, block_counts, first_block, block_total):
    block_ids = first_block + jnp.arange(block_total, dtype=jnp.int32)
    valid_entry = jnp.arange(block_lists.shape[1], dtype=jnp.int32)[None, :] < block_counts[:, None]
    entry_hits = (block_lists[:, :, None] == block_ids[None, None, :]) & valid_entry[:, :, None]
    return jnp.repeat(jnp.any(entry_hits, axis=1).astype(jnp.float32), BLK, axis=1)


def per_device(anc_inverse, l_store, diag_inv, block_lists, block_counts, sibling_columns):
    row_cells = anc_inverse.shape[0]
    col_cells = anc_inverse.shape[1]
    col_count = lax.axis_size("col")
    row_index = lax.axis_index(ROW)
    col_index = lax.axis_index("col")
    row_mask = listed_blocks(
        block_lists, block_counts, row_index * (row_cells // BLK), row_cells // BLK
    )
    col_mask = listed_blocks(
        block_lists, block_counts, col_index * (col_cells // BLK), col_cells // BLK
    )
    own_slot = l_store[0]
    chosen = (sibling_columns == col_index).astype(jnp.float32)
    placed = chosen[:, None, None] * own_slot[None]
    stacked = total_of(placed, "col")
    masked = stacked * row_mask[:, :, None]
    partial_value = (
        -jnp.einsum(
            "jrw,rc->jwc",
            masked,
            anc_inverse,
            precision=lax.Precision.HIGHEST,
            preferred_element_type=jnp.float32,
        )
        * col_mask[:, None, :]
    )
    upper_part = summed_rows(partial_value, ROW, 1)
    owner_table = (
        sibling_columns[:, None] == jnp.arange(col_count, dtype=jnp.int32)[None, :]
    ).astype(jnp.float32)
    slots = jnp.einsum(
        "jc,jwt->wct",
        owner_table,
        upper_part,
        precision=lax.Precision.HIGHEST,
        preferred_element_type=jnp.float32,
    )
    slots = slots.reshape(slots.shape[0], col_count * col_cells)
    by_owner = lax.all_to_all(slots, "col", split_axis=1, concat_axis=1, tiled=True)
    picked = lax.all_to_all(by_owner, ROW, split_axis=1, concat_axis=0, tiled=True)
    own_panel = jnp.sum(chosen[:, None, None] * masked, axis=0)
    inner_sum = jnp.dot(
        picked, own_panel, precision=lax.Precision.HIGHEST, preferred_element_type=jnp.float32
    )
    diag_total = nested_sum(inner_sum, ROW)
    present = jnp.sum(chosen)
    diag_out = (present * diag_inv[0] - diag_total)[None]
    lower_out = jnp.transpose(picked)[None]
    return (upper_part, lower_out, diag_out)


def solution(mesh):
    finer = Mesh(mesh.devices.reshape(8, 2, mesh.shape["col"]), ("row_0", "row_1", "col"))
    return jax.shard_map(
        per_device,
        mesh=finer,
        in_specs=(P(ROW, "col"), P("col", ROW, None), P("col", None, None), P(), P(), P()),
        out_specs=(P(None, ROW, "col"), P("col", ROW, None), P("col", None, None)),
        check_vma=False,
    )
```

profile of v0, /device:TPU:2, one launch (start us, length us, event | category | flops | bytes accessed | tf_op | source)
XLA Modules:
  0.0 359.1 jit_solution(242088408683245852)
XLA Ops:
  7.2 1.3 fusion.15
  8.6 4.4 %bitcast_multiply_fusion = f32[5120,256]{1,0:T(8,128)} fusion(f32[1280,256]{1,0:T(8,128)} %bitcast.42, f32[5120]{0:T(1024)S(1)} %mul.67), kind=kLoop, calls=%fused_computation.2 | loop fusion | flops 1310720 | bytes 6574080 | tf_op jit(solution)/shard_map/mul | solution.py:86
  13.1 70.1 %reduce-scatter.4.cloned.1.call-done = f32[320,256]{1,0:T(8,128)} async-done(((f32[5120,256]{1,0:T(8,128)}), f32[320,256]{1,0:T(8,128)}) %reduce-scatter.4.cloned.1.call-update) | async-done | bytes 327696 | tf_op jit(solution)/shard_map/reduce_scatter | solution.py:19
  83.4 0.5 and_reduce_fusion.1
  83.9 0.1 copy.32
  84.1 0.1 copy.34
  84.3 44.9 %all-gather.2.cloned.1.call-done = f32[5120,256]{1,0:T(8,128)} async-done(((f32[320,256]{1,0:T(8,128)}), f32[5120,256]{1,0:T(8,128)}) %all-gather.2.cloned.1.call-update) | async-done | bytes 5242896 | tf_op jit(solution)/shard_map/all_gather | solution.py:20
  129.2 28.0 %negate_multiply_fusion = f32[4,256,1280]{2,1,0:T(8,128)} fusion(f32[1280,1280]{1,0:T(8,128)} %param.6, f32[4,1280,256]{2,1,0:T(8,128)} %bitcast.40, f32[4,1280]{1,0:T(4,128)S(1)} %bitcast.46, f32[4,1280]{1,0:T(4,128)S(1)} %bitcast.44), kind=kOutput, calls=%fused_computation.4 | convolution fusion | flops 20136591360 | bytes 17080320 | tf_op jit(solution)/shard_map/jrw,rc->jwc/dot_general | solution.py:90
  157.2 0.2 reduce-scatter.8.cloned.1.call-start
  157.4 66.1 %reduce-scatter.6.cloned.1.call-done = f32[4,32,1280]{2,1,0:T(8,128)} async-done(((f32[4,256,1280]{2,1,0:T(8,128)}), f32[4,32,1280]{2,1,0:T(8,128)}) %reduce-scatter.6.cloned.1.call-update) | async-done | bytes 655376 | tf_op jit(solution)/shard_map/reduce_scatter | solution.py:27
  223.5 24.2 %reduce-scatter.8.cloned.1.call-done = f32[4,16,1280]{2,1,0:T(8,128)} async-done(((f32[4,32,1280]{2,1,0:T(8,128)}), f32[4,16,1280]{2,1,0:T(8,128)}) %reduce-scatter.8.cloned.1.call-update) | async-done | bytes 327696 | tf_op jit(solution)/shard_map/reduce_scatter | solution.py:27
  247.7 1.8 convolution_bitcast_fusion
  249.5 0.8 copy.36
  250.3 21.4 %all_to_all.32 = f32[16,16,1280]{2,0,1:T(8,128)} all-to-all(f32[16,16,1280]{2,0,1:T(8,128)S(1)} %copy.36), channel_id=1, replica_groups=mesh['row_0'=8,'row_1'=2,'col'=16] {'col'}, dimensions={1} | all-to-all | bytes 2621440 | tf_op jit(solution)/shard_map/all_to_all | solution.py:111
  271.7 8.6 %all-to-all-start.1 = ((f32[16,16,1280]{2,0,1:T(8,128)}), f32[16,16,1280]{2,0,1:T(8,128)S(1)}, u32[]{:S(2)}, u32[]{:S(2)}) async-start(f32[16,16,1280]{2,0,1:T(8,128)} %all_to_all.32), calls=%async_computation.4 | async-start | bytes 2621440 | tf_op jit(solution)/shard_map/all_to_all | solution.py:112
  280.3 3.1 multiply_reduce_fusion
  283.4 33.1 %all-to-all-done.1 = f32[16,16,1280]{2,0,1:T(8,128)S(1)} async-done(((f32[16,16,1280]{2,0,1:T(8,128)}), f32[16,16,1280]{2,0,1:T(8,128)S(1)}, u32[]{:S(2)}, u32[]{:S(2)}) %all-to-all-start.1) | async-done | bytes 1310752 | tf_op jit(solution)/shard_map/all_to_all | solution.py:112
  316.5 1.2 fusion.8
  317.8 17.0 %all_to_all.33 = f32[16,16,256]{2,1,0:T(8,128)S(1)} all-to-all(f32[16,16,256]{2,1,0:T(8,128)S(1)} %fusion.8), channel_id=1, replica_groups=mesh['row_0'=8,'row_1'=2,'col'=16] {'row_0','row_1'}, dimensions={0} | all-to-all | bytes 524288 | tf_op jit(solution)/shard_map/all_to_all | solution.py:54
  334.8 0.7 broadcast_in_dim.11
  335.5 3.5 all-to-all-start.3
  339.1 1.5 copy.37
  340.5 10.7 %all-to-all-done.3 = f32[16,16,256]{2,1,0:T(8,128)S(1)} async-done(((f32[16,16,256]{2,1,0:T(8,128)}), f32[16,16,256]{2,1,0:T(8,128)S(1)}, u32[]{:S(2)}, u32[]{:S(2)}) %all-to-all-start.3) | async-done | bytes 262176 | tf_op jit(solution)/shard_map/all_to_all | solution.py:39
  351.2 1.3 bitcast_subtract_fusion
  (26 shorter events, 0.6 us)
Async XLA Ops:
  7.2 76.0 %reduce-scatter.4.cloned.1.call-start = ((), (), s32[]{:S(2)}) async-start(), calls=%async_computation.7 | async-start | bytes 5570560 | tf_op jit(solution)/shard_map/reduce_scatter | solution.py:19
  8.6 74.7 %copy-start.3 = (s32[4]{0:T(128)S(1)}, s32[4]{0:T(128)}, u32[]{:S(2)}) copy-start(s32[4]{0:T(128)} %param.10) | copy-start | bytes 52
  8.6 74.8 %copy-start.2 = (s32[4,96]{1,0:T(4,128)S(1)}, s32[4,96]{1,0:T(4,128)}, u32[]{:S(2)}) copy-start(s32[4,96]{1,0:T(4,128)} %param.9) | copy-start | bytes 4612
  13.0 116.1 %all-gather.2.cloned.1.call-start = ((), (), s32[]{:S(2)}) async-start(), calls=%async_computation.8 | async-start | bytes 5570560 | tf_op jit(solution)/shard_map/all_gather | solution.py:20
  83.2 140.3 %reduce-scatter.6.cloned.1.call-start = ((), (), s32[]{:S(2)}) async-start(), calls=%async_computation.9 | async-start | bytes 5898240 | tf_op jit(solution)/shard_map/reduce_scatter | solution.py:27
  157.2 90.5 %copy-start.1 = (s32[4]{0:T(128)S(1)}, s32[4]{0:T(128)}, u32[]{:S(2)}) copy-start(s32[4]{0:T(128)} %param.11) | copy-start | bytes 52
  157.2 90.5 %reduce-scatter.8.cloned.1.call-start = ((), (), s32[]{:S(2)}) async-start(), calls=%async_computation.10 | async-start | bytes 983040 | tf_op jit(solution)/shard_map/reduce_scatter | solution.py:27
  271.7 44.8 %all-to-all-start.1 = ((f32[16,16,1280]{2,0,1:T(8,128)}), f32[16,16,1280]{2,0,1:T(8,128)S(1)}, u32[]{:S(2)}, u32[]{:S(2)}) async-start(f32[16,16,1280]{2,0,1:T(8,128)} %all_to_all.32), calls=%async_computation.4 | async-start | bytes 2621440 | tf_op jit(solution)/shard_map/all_to_all | solution.py:112
  280.3 70.9 %copy-start = (f32[1,256,256]{2,1,0:T(8,128)S(1)}, f32[1,256,256]{2,1,0:T(8,128)}, u32[]{:S(2)}) copy-start(f32[1,256,256]{2,1,0:T(8,128)} %param.8) | copy-start | bytes 786436
  335.5 15.7 %all-to-all-start.3 = ((f32[16,16,256]{2,1,0:T(8,128)}), f32[16,16,256]{2,1,0:T(8,128)S(1)}, u32[]{:S(2)}, u32[]{:S(2)}) async-start(f32[16,16,256]{2,1,0:T(8,128)} %broadcast_in_dim.11), calls=%async_computation.6 | async-start | bytes 524288 | tf_op jit(solution)/shard_map/all_to_all | solution.py:39
Sparse Core Ops, SparseCore 0:
  13.1 70.0 reduce-scatter.3
  85.0 44.0 all-gather.1
  157.3 66.1 reduce-scatter.5
  226.4 21.2 reduce-scatter.7
where the time goes:
time: 360 us; the launch traced here: 359 us
  waiting for transfers between devices  249 us (69%)
  blocking collectives  38.4 us (11%)
  matrix products  31.1 us (9%)
  between operations  13.9 us (4%)
  starting transfers between devices  12.5 us (3%)
  other arithmetic  10.7 us (3%)
    reduce_scatter x2, waiting for transfers between devices, summed_rows(): nearer = lax.psum_scatter(x, axes[0], scatter_dimension=dim, tiled=True)  90.2 us
    reduce_scatter x1, waiting for transfers between devices, total_of(): own = lax.psum_scatter(padded, axis, scatter_dimension=0, tiled=True)  70.1 us
    all_gather x1, waiting for transfers between devices, total_of(): whole = lax.all_gather(own, axis, axis=0, tiled=True)  44.9 us
    all_to_all x1, waiting for transfers between devices, per_device(): lax.all_to_all(by_owner, ROW, split_axis=1, concat_axis=0, tiled=True)  33.1 us
    dot_general x1, matrix products, per_device(): jnp.einsum('jrw,rc->jwc', masked, anc_inverse, precision=lax.Precision.HI...  28 us
    all_to_all x1, blocking collectives, per_device(): lax.all_to_all(slots, 'col', split_axis=1, concat_axis=1, tiled=True)  21.4 us
    all_to_all x1, blocking collectives, sum_at_owner(): parts = lax.all_to_all(cut_along(x, dim, length), axis, 0, 0, tiled=True)  17 us
    all_to_all x1, waiting for transfers between devices, from_everyone(): lax.all_to_all(jnp.broadcast_to(x[None], (length, *x.shape)), axis, 0, 0,...  10.7 us
  transfers between devices with their start and end apart: 6, of which 6 were waited for; matrix products, arithmetic and copies ran while one was open for 2% of the time, Pallas kernels for 0%

commit v1 on v0

--- a/solution.py
+++ b/solution.py
@@ -6,6 +6,13 @@
 
 BLK = 128
 ROW = ("row_0", "row_1")
+
+
+def all_by_exchange(array, axis, d):
+    size = lax.axis_size(axis)
+    blocks = jnp.stack([array for _ in range(size)])
+    blocks = lax.all_to_all(blocks, axis, split_axis=0, concat_axis=0)
+    return jnp.concatenate(blocks, axis=d)
 
 
 def padded_to(lines, length):
@@ -17,7 +24,7 @@
     lines = x.reshape(-1, *x.shape[1:][-1:])
     padded = padded_to(lines, lax.axis_size(axis))
     own = lax.psum_scatter(padded, axis, scatter_dimension=0, tiled=True)
-    whole = lax.all_gather(own, axis, axis=0, tiled=True)
+    whole = all_by_exchange(own, axis, 0)
     return whole[: len(lines)].reshape(x.shape)
 
 

time: 360 us -> 417 us (1.16)
  blocking collectives: 38.4 us -> 83 us
  matrix products: 31.1 us -> 48.4 us
  waiting for transfers between devices: 249 us -> 240 us
    all_to_all x0 -> x1, blocking collectives: none -> 45.7 us  [per_device(): lax.all_to_all(by_owner, ROW, split_axis=1, concat_axis=0, tiled=True)]
    all_gather x1 -> x0, waiting for transfers between devices: 44.9 us -> none  [total_of(): whole = lax.all_gather(own, axis, axis=0, tiled=True)]
    all_to_all x1, waiting for transfers between devices: 33.1 us -> 69.9 us  [all_by_exchange(): blocks = lax.all_to_all(blocks, axis, split_axis=0, concat_axis=0)]
    dot_general x1, matrix products: 28 us -> 45.4 us  [per_device(): jnp.einsum('jrw,rc->jwc', masked, anc_inverse, precision=lax.Precision.HI...]
  transfers between devices with their start and end apart: 6 -> 5, of which waited for: 6 -> 5; matrix products, arithmetic and copies ran while one was open for 2% -> 1% of each run, Pallas kernels for 0% -> 0%
where the time goes in v1:
time: 417 us; the launch traced here: 416 us
  waiting for transfers between devices  240 us (58%)
  blocking collectives  83 us (20%)
  matrix products  48.4 us (12%)
  between operations  13.8 us (3%)
  starting transfers between devices  13.1 us (3%)
  other arithmetic  10.8 us (3%)
  local copies, waits for them, and re-layouts  7.24 us (2%)
    reduce_scatter x2, waiting for transfers between devices, summed_rows(): nearer = lax.psum_scatter(x, axes[0], scatter_dimension=dim, tiled=True)  88.9 us
    reduce_scatter x1, waiting for transfers between devices, total_of(): own = lax.psum_scatter(padded, axis, scatter_dimension=0, tiled=True)  70.2 us
    all_to_all x1, waiting for transfers between devices, all_by_exchange(): blocks = lax.all_to_all(blocks, axis, split_axis=0, concat_axis=0)  69.9 us
    all_to_all x1, blocking collectives, per_device(): lax.all_to_all(by_owner, ROW, split_axis=1, concat_axis=0, tiled=True)  45.7 us
    dot_general x1, matrix products, per_device(): jnp.einsum('jrw,rc->jwc', masked, anc_inverse, precision=lax.Precision.HI...  45.4 us
    all_to_all x1, blocking collectives, per_device(): lax.all_to_all(slots, 'col', split_axis=1, concat_axis=1, tiled=True)  21.3 us
    all_to_all x1, blocking collectives, sum_at_owner(): parts = lax.all_to_all(cut_along(x, dim, length), axis, 0, 0, tiled=True)  16 us
    all_to_all x1, waiting for transfers between devices, from_everyone(): lax.all_to_all(jnp.broadcast_to(x[None], (length, *x.shape)), axis, 0, 0,...  10.7 us
  transfers between devices with their start and end apart: 5, of which 5 were waited for; matrix products, arithmetic and copies ran while one was open for 1% of the time, Pallas kernels for 0%

profile of v1, /device:TPU:2, one launch (start us, length us, event | category | flops | bytes accessed | tf_op | source)
XLA Modules:
  0.0 416.2 jit_solution(5093060180059555187)
XLA Ops:
  7.2 1.3 fusion.11
  8.6 4.4 %bitcast_multiply_fusion.1 = f32[5120,256]{1,0:T(8,128)} fusion(f32[1280,256]{1,0:T(8,128)} %bitcast.43, f32[5120]{0:T(1024)S(1)} %mul.67), kind=kLoop, calls=%fused_computation.3 | loop fusion | flops 1310720 | bytes 6574080 | tf_op jit(solution)/shard_map/mul | solution.py:93
  13.0 70.2 %reduce-scatter.4.cloned.1.call-done = f32[320,256]{1,0:T(8,128)} async-done(((f32[5120,256]{1,0:T(8,128)}), f32[320,256]{1,0:T(8,128)}) %reduce-scatter.4.cloned.1.call-update) | async-done | bytes 327696 | tf_op jit(solution)/shard_map/reduce_scatter | solution.py:26
  83.2 3.8 stack.2
  87.0 9.2 %all-to-all-start = ((f32[16,320,256]{2,1,0:T(8,128)}), f32[16,320,256]{2,1,0:T(8,128)}, u32[]{:S(2)}, u32[]{:S(2)}) async-start(f32[16,320,256]{2,1,0:T(8,128)} %stack.2), calls=%async_computation.1 | async-start | bytes 10485760 | tf_op jit(solution)/shard_map/all_to_all | solution.py:14
  96.4 0.5 and_reduce_fusion
  96.9 0.1 copy.32
  97.3 69.9 %all-to-all-done = f32[16,320,256]{2,1,0:T(8,128)} async-done(((f32[16,320,256]{2,1,0:T(8,128)}), f32[16,320,256]{2,1,0:T(8,128)}, u32[]{:S(2)}, u32[]{:S(2)}) %all-to-all-start) | async-done | bytes 5242912 | tf_op jit(solution)/shard_map/all_to_all | solution.py:14
  167.2 3.1 multiply_reduce_fusion
  170.3 45.4 %negate_multiply_fusion = f32[4,256,1280]{2,1,0:T(8,128)} fusion(f32[4,1280,256]{2,1,0:T(8,128)S(1)} %get-tuple-element.23, f32[1280,1280]{1,0:T(8,128)} %param.6, f32[4,1280]{1,0:T(4,128)S(1)} %bitcast.46), kind=kOutput, calls=%fused_computation.5 | convolution fusion | flops 20135280640 | bytes 17059840 | tf_op jit(solution)/shard_map/jrw,rc->jwc/dot_general | solution.py:97
  215.7 0.2 reduce-scatter.8.cloned.1.call-start
  216.0 64.6 %reduce-scatter.6.cloned.1.call-done = f32[4,32,1280]{2,1,0:T(8,128)} async-done(((f32[4,256,1280]{2,1,0:T(8,128)}), f32[4,32,1280]{2,1,0:T(8,128)}) %reduce-scatter.6.cloned.1.call-update) | async-done | bytes 655376 | tf_op jit(solution)/shard_map/reduce_scatter | solution.py:34
  280.6 24.3 %reduce-scatter.8.cloned.1.call-done = f32[4,16,1280]{2,1,0:T(8,128)} async-done(((f32[4,32,1280]{2,1,0:T(8,128)}), f32[4,16,1280]{2,1,0:T(8,128)}) %reduce-scatter.8.cloned.1.call-update) | async-done | bytes 327696 | tf_op jit(solution)/shard_map/reduce_scatter | solution.py:34
  304.9 1.8 convolution_bitcast_fusion
  306.8 0.8 copy.36
  307.5 21.3 %all_to_all.37 = f32[16,16,1280]{2,0,1:T(8,128)S(1)} all-to-all(f32[16,16,1280]{2,0,1:T(8,128)S(1)} %copy.36), channel_id=1, replica_groups=mesh['row_0'=8,'row_1'=2,'col'=16] {'col'}, dimensions={1} | all-to-all | bytes 2621440 | tf_op jit(solution)/shard_map/all_to_all | solution.py:118
  328.8 45.7 %all_to_all.38 = f32[16,16,1280]{2,0,1:T(8,128)S(1)} all-to-all(f32[16,16,1280]{2,0,1:T(8,128)S(1)} %all_to_all.37), channel_id=1, replica_groups=mesh['row_0'=8,'row_1'=2,'col'=16] {'row_0','row_1'}, dimensions={1} | all-to-all | bytes 2621440 | tf_op jit(solution)/shard_map/all_to_all | solution.py:119
  374.6 1.2 fusion.4
  375.8 16.0 %all_to_all.39 = f32[16,16,256]{2,1,0:T(8,128)S(1)} all-to-all(f32[16,16,256]{2,1,0:T(8,128)S(1)} %fusion.4), channel_id=1, replica_groups=mesh['row_0'=8,'row_1'=2,'col'=16] {'row_0','row_1'}, dimensions={0} | all-to-all | bytes 524288 | tf_op jit(solution)/shard_map/all_to_all | solution.py:61
  391.8 0.7 broadcast_in_dim.11
  392.6 3.5 all-to-all-start.4
  396.1 1.5 copy.37
  397.6 10.7 %all-to-all-done.4 = f32[16,16,256]{2,1,0:T(8,128)S(1)} async-done(((f32[16,16,256]{2,1,0:T(8,128)}), f32[16,16,256]{2,1,0:T(8,128)S(1)}, u32[]{:S(2)}, u32[]{:S(2)}) %all-to-all-start.4) | async-done | bytes 262176 | tf_op jit(solution)/shard_map/all_to_all | solution.py:46
  408.3 1.4 bitcast_subtract_fusion
  (25 shorter events, 0.6 us)
Async XLA Ops:
  7.2 76.0 %reduce-scatter.4.cloned.1.call-start = ((), (), s32[]{:S(2)}) async-start(), calls=%async_computation.8 | async-start | bytes 5570560 | tf_op jit(solution)/shard_map/reduce_scatter | solution.py:26
  87.0 9.3 %copy-start.3 = (s32[4]{0:T(128)S(1)}, s32[4]{0:T(128)}, u32[]{:S(2)}) copy-start(s32[4]{0:T(128)} %param.10) | copy-start | bytes 52
  87.0 9.4 %copy-start.2 = (s32[4,96]{1,0:T(4,128)S(1)}, s32[4,96]{1,0:T(4,128)}, u32[]{:S(2)}) copy-start(s32[4,96]{1,0:T(4,128)} %param.9) | copy-start | bytes 4612
  87.0 80.3 %all-to-all-start = ((f32[16,320,256]{2,1,0:T(8,128)}), f32[16,320,256]{2,1,0:T(8,128)}, u32[]{:S(2)}, u32[]{:S(2)}) async-start(f32[16,320,256]{2,1,0:T(8,128)} %stack.2), calls=%async_computation.1 | async-start | bytes 10485760 | tf_op jit(solution)/shard_map/all_to_all | solution.py:14
  96.2 184.3 %reduce-scatter.6.cloned.1.call-start = ((), (), s32[]{:S(2)}) async-start(), calls=%async_computation.9 | async-start | bytes 5898240 | tf_op jit(solution)/shard_map/reduce_scatter | solution.py:34
  215.7 89.2 %copy-start.1 = (s32[4]{0:T(128)S(1)}, s32[4]{0:T(128)}, u32[]{:S(2)}) copy-start(s32[4]{0:T(128)} %param.11) | copy-start | bytes 52
  215.7 89.2 %reduce-scatter.8.cloned.1.call-start = ((), (), s32[]{:S(2)}) async-start(), calls=%async_computation.10 | async-start | bytes 983040 | tf_op jit(solution)/shard_map/reduce_scatter | solution.py:34
  328.8 79.5 %copy-start = (f32[1,256,256]{2,1,0:T(8,128)S(1)}, f32[1,256,256]{2,1,0:T(8,128)}, u32[]{:S(2)}) copy-start(f32[1,256,256]{2,1,0:T(8,128)} %param.8) | copy-start | bytes 786436
  392.6 15.7 %all-to-all-start.4 = ((f32[16,16,256]{2,1,0:T(8,128)}), f32[16,16,256]{2,1,0:T(8,128)S(1)}, u32[]{:S(2)}, u32[]{:S(2)}) async-start(f32[16,16,256]{2,1,0:T(8,128)} %broadcast_in_dim.11), calls=%async_computation.7 | async-start | bytes 524288 | tf_op jit(solution)/shard_map/all_to_all | solution.py:46
Sparse Core Ops, SparseCore 0:
  13.1 70.0 reduce-scatter.3
  215.9 64.6 reduce-scatter.5
  283.6 21.2 reduce-scatter.7
